TPU v7x, 256 devices: a whole 4x4x8 slice. The times are simulated.
256 devices in a mesh: rx: 16 (over x, z_lo), ry: 16 (over z_hi, y, core).
Axes of the slice: x: 4, y: 4, z: 8 (z_hi: 2, z_lo: 4; z = z_hi * 4 + z_lo), core: 2. Of those that a mesh axis runs over, the one named last changes fastest.
Arguments:
- clean: bfloat16 [16, 16, 4, 2, 192, 1024], P('rx', 'ry'), may hold values from -6 to 6
- noise: bfloat16 [16, 16, 4, 2, 192, 1024], P('rx', 'ry'), may hold values from -6 to 6
- noise_level: int32 [16, 16, 4, 2], P('rx', 'ry'), may hold values from 0 to 31
- weight: float32 [16, 16, 9, 192, 192], P('rx', 'ry'), may hold values from -6 to 6
- velocity: float32 [16, 16, 9, 192, 192], P('rx', 'ry'), may hold values from -0.6 to 0.6
Outputs:
- new_weight: float32 [16, 16, 9, 192, 192], P('rx', 'ry')
- new_velocity: float32 [16, 16, 9, 192, 192], P('rx', 'ry')
All inputs are finite; a program needn't handle non-finite values.
Results may differ from a plain program's by a relative error of at most 0.0066.
Values sent between devices are 32-bit elements; how exact they have to be, the bound alone decides.
A program may use at most 192 MiB of HBM per device.

v0:
```python
import math

import jax
import jax.numpy as jnp
from jax import lax
from jax.experimental import pallas as pl
from jax.experimental.pallas import tpu as pltpu
from jax.sharding import PartitionSpec as P

RES = 32
CELLS = RES * RES
STEPS = 4
LEVELS = 32
C = 192
TAPS = 9
FAN = TAPS * C
OC = 16
HALF = OC // 2
ROWS = OC + HALF
CHUNKS = C // OC
BATCH = 2

norm_epsilon = 1e-05
momentum_decay = 0.9
learn_rate = 50.0
silu_scale = 0.596
MESH = pl.DeviceIdType.MESH
F32 = jnp.float32
BF16 = jnp.bfloat16


def partner_of(step):
    rx, ry = lax.axis_index("rx"), lax.axis_index("ry")
    odd = step % 2
    bit_x = (8 - 2 * step) * (1 - odd)
    bit_y = (10 - 2 * step) * odd
    px = rx + bit_x * (1 - 2 * ((rx // (bit_x + odd)) % 2))
    py = ry + bit_y * (1 - 2 * ((ry // (bit_y + 1 - odd)) % 2))
    return {"rx": px, "ry": py}


def pack(full):
    rest = full[:, :, 128:]
    return full[:, :, :128], jnp.concatenate([rest[:, :HALF], rest[:, HALF:]], axis=-1)


def unpack(packed):
    rest = packed[:, OC:]
    rest = jnp.concatenate([rest[:, :, :64], pltpu.roll(rest, 64, 2)[:, :, :64]], axis=1)
    return jnp.concatenate([packed[:, :OC], rest], axis=-1)


def roll_cells(array, by):
    return pltpu.roll(array, by % CELLS, 1)


def kernel(
    level_ref, clean_hbm, noise_hbm, w_hbm, v_hbm, new_w_hbm, new_v_hbm,
    clean, noise, w_in, v_in, x_ref, xt_ref, mine, other, vel, w_out, v_out,
    in_sem, wv_sem, out_sem, send_sem, recv_sem,
):
    pltpu.make_async_copy(w_hbm.at[0, 0], w_in, wv_sem.at[0]).start()
    pltpu.make_async_copy(v_hbm.at[0, 0], v_in, wv_sem.at[1]).start()
    for step in range(STEPS):
        pltpu.make_async_copy(clean_hbm.at[0, 0, step], clean.at[step], in_sem.at[0, step]).start()
        pltpu.make_async_copy(noise_hbm.at[0, 0, step], noise.at[step], in_sem.at[1, step]).start()

    barrier = pltpu.get_barrier_semaphore()
    for step in range(STEPS):
        pl.semaphore_signal(barrier, inc=1, device_id=partner_of(step), device_id_type=MESH)

    pltpu.make_async_copy(w_hbm.at[0, 0], w_in, wv_sem.at[0]).wait()
    pltpu.make_async_copy(v_hbm.at[0, 0], v_in, wv_sem.at[1]).wait()

    def turn(tap, carry):
        wt = jnp.transpose(w_in[tap])
        rest = wt[:, 128:].reshape(CHUNKS, 2, HALF, 64)
        rest = jnp.concatenate([rest[:, 0], rest[:, 1]], axis=-1)
        for slot in (mine, other):
            slot[0, :, tap, :OC, :] = wt[:, :128].reshape(CHUNKS, OC, 128)
            slot[0, :, tap, OC:, :] = rest
        vel[tap] = jnp.transpose(v_in[tap])
        return carry

    lax.fori_loop(0, TAPS, turn, 0)

    pl.semaphore_wait(barrier, STEPS)

    lane = lax.broadcasted_iota(jnp.int32, (1, CELLS), 1)
    row, col = lane // RES, lane % RES
    ok_row = {-1: row > 0, 1: row < RES - 1}
    ok_col = {-1: col > 0, 1: col < RES - 1}

    def prepare(step):
        pltpu.make_async_copy(clean_hbm.at[0, 0, step], clean.at[step], in_sem.at[0, step]).wait()
        pltpu.make_async_copy(noise_hbm.at[0, 0, step], noise.at[step], in_sem.at[1, step]).wait()
        for b in range(BATCH):
            level = jnp.full((1, 128), level_ref[0, 0, step, b].astype(F32), F32)
            sigma = 0.2 * jnp.exp(level * (math.log(25.0) / (LEVELS - 1)))
            c_in = 1.0 / jnp.sqrt(sigma * sigma + 0.25)

            def block(i, carry):
                at = pl.multiple_of(i * 128, 128)
                noisy = c_in * (
                    clean[step, b, :, pl.ds(at, 128)].astype(F32)
                    + sigma * noise[step, b, :, pl.ds(at, 128)].astype(F32)
                )
                x_ref[step, b, :, pl.ds(at, 128)] = noisy.astype(BF16)
                xt_ref[step, b, pl.ds(at, 128), :] = jnp.transpose(noisy).astype(BF16)
                return carry

            lax.fori_loop(0, CELLS // 128, block, 0)

    def exchange(step, chunk):
        return pltpu.make_async_remote_copy(
            src_ref=mine.at[step + 1, chunk],
            dst_ref=other.at[step + 1, chunk],
            send_sem=send_sem.at[step, chunk],
            recv_sem=recv_sem.at[step, chunk],
            device_id=partner_of(step),
            device_id_type=MESH,
        )

    def task(step, chunk):
        at = pl.multiple_of(chunk * OC, OC)

        @pl.when(step > 0)
        def _():
            exchange(step - 1, chunk).wait_recv()

        w = unpack(0.5 * (mine[step, chunk] + other[step, chunk]))
        square = jnp.sum(jnp.sum(w * w, axis=0), axis=1, keepdims=True)
        radius = jnp.sqrt(square / FAN + norm_epsilon)
        scale = 1.0 / (radius * math.sqrt(FAN))
        lhs = (w * scale).astype(BF16).reshape(TAPS * OC, C)
        grad_eff = jnp.zeros((TAPS * OC, C), F32)
        for b in range(BATCH):
            y = jnp.dot(lhs, x_ref[step, b], preferred_element_type=F32)
            tap = lambda dy, dx: y[(3 * (dy + 1) + dx + 1) * OC :][:OC]
            z = None
            for dx in (0, -1, 1):
                part = tap(0, dx)
                for dy in (-1, 1):
                    part = part + jnp.where(ok_row[dy], roll_cells(tap(dy, dx), -RES * dy), 0.0)
                z = part if dx == 0 else z + jnp.where(ok_col[dx], roll_cells(part, -dx), 0.0)
            sig = 1.0 / (1.0 + jnp.exp(-z))
            error = z * sig * (1.0 / silu_scale) - clean[step, b, pl.ds(at, OC), :].astype(F32)
            dz = error * sig * (1.0 + z * (1.0 - sig)) * (2.0 / (silu_scale * BATCH * CELLS))
            dz = dz.astype(BF16).astype(F32)
            pieces = {}
            for dx in (0, -1, 1):
                moved = dz if dx == 0 else roll_cells(jnp.where(ok_col[dx], dz, 0.0), dx)
                for dy in (0, -1, 1):
                    piece = (
                        moved if dy == 0 else roll_cells(jnp.where(ok_row[dy], moved, 0.0), RES * dy)
                    )
                    pieces[dy, dx] = piece.astype(BF16)
            rows = jnp.concatenate(
                [pieces[dy, dx] for dy in (-1, 0, 1) for dx in (-1, 0, 1)], axis=0
            )
            grad_eff += jnp.dot(rows, xt_ref[step, b], preferred_element_type=F32)
        grad_eff = grad_eff.reshape(TAPS, OC, C)
        inner = jnp.sum(jnp.sum(grad_eff * w, axis=0), axis=1, keepdims=True)
        back = inner / (FAN * math.sqrt(FAN) * (radius * radius * radius))
        grad = grad_eff * scale - w * back
        v = momentum_decay * vel[:, pl.ds(at, OC), :] + learn_rate * grad
        vel[:, pl.ds(at, OC), :] = v
        first, rest = pack(w - v)
        mine[step + 1, chunk, :, :OC, :] = first
        mine[step + 1, chunk, :, OC:, :] = rest
        exchange(step, chunk).start()

        @pl.when(step == STEPS - 1)
        def _():
            write(vel, new_v_hbm, 1, chunk).start()

    def write(src, dst, which, chunk):
        at = pl.multiple_of(chunk * OC, OC)
        return pltpu.make_async_copy(
            src.at[:, pl.ds(at, OC), :], dst.at[:, pl.ds(at, OC), :], out_sem.at[which, chunk]
        )

    def finish(chunk):
        at = pl.multiple_of(chunk * OC, OC)
        exchange(STEPS - 1, chunk).wait_recv()
        w_out[:, pl.ds(at, OC), :] = unpack(0.5 * (mine[STEPS, chunk] + other[STEPS, chunk]))
        write(w_out, new_w_hbm, 0, chunk).start()

    def wave(k, carry):
        @pl.when(k < STEPS)
        def _():
            prepare(k)

        def inner(step, carry):
            chunk = k - step - step // 2

            @pl.when((chunk >= 0) & (chunk < CHUNKS))
            def _():
                task(step, chunk)

            return carry

        lax.fori_loop(0, STEPS, inner, 0)

        @pl.when(k >= 5)
        def _():
            finish(k - 5)

        return carry

    lax.fori_loop(0, CHUNKS + 5, wave, 0)

    def drain(chunk, carry):
        for step in range(STEPS):
            exchange(step, chunk).wait_send()
        write(w_out, new_w_hbm, 0, chunk).wait()
        write(vel, new_v_hbm, 1, chunk).wait()
        return carry

    lax.fori_loop(0, CHUNKS, drain, 0)


def body(clean, noise, noise_level, weight, velocity):
    hbm = pl.BlockSpec(memory_space=pl.ANY)
    out = jax.ShapeDtypeStruct((TAPS, C, C), F32)
    new_w, new_v = pl.pallas_call(
        kernel,
        out_shape=(out, out),
        in_specs=[pl.BlockSpec(memory_space=pltpu.SMEM), hbm, hbm, hbm, hbm],
        out_specs=(hbm, hbm),
        scratch_shapes=[
            pltpu.VMEM((STEPS, BATCH, C, CELLS), BF16),
            pltpu.VMEM((STEPS, BATCH, C, CELLS), BF16),
            pltpu.VMEM((TAPS, C, C), F32),
            pltpu.VMEM((TAPS, C, C), F32),
            pltpu.VMEM((STEPS, BATCH, C, CELLS), BF16),
            pltpu.VMEM((STEPS, BATCH, CELLS, C), BF16),
            pltpu.VMEM((STEPS + 1, CHUNKS, TAPS, ROWS, 128), F32),
            pltpu.VMEM((STEPS + 1, CHUNKS, TAPS, ROWS, 128), F32),
            pltpu.VMEM((TAPS, C, C), F32),
            pltpu.VMEM((TAPS, C, C), F32),
            pltpu.VMEM((8, 128), F32),
            pltpu.SemaphoreType.DMA((2, STEPS)),
            pltpu.SemaphoreType.DMA((2,)),
            pltpu.SemaphoreType.DMA((2, CHUNKS)),
            pltpu.SemaphoreType.DMA((STEPS, CHUNKS)),
            pltpu.SemaphoreType.DMA((STEPS, CHUNKS)),
        ],
        compiler_params=pltpu.CompilerParams(
            collective_id=0, has_side_effects=True, vmem_limit_bytes=58 << 20
        ),
        name="train",
    )(noise_level, clean, noise, weight, velocity)
    return (
        jnp.swapaxes(new_w, 1, 2)[None, None],
        jnp.swapaxes(new_v, 1, 2)[None, None],
    )


def solution(mesh):
    in_specs = (
        P("rx", "ry", None, None, None, None),
        P("rx", "ry", None, None, None, None),
        P("rx", "ry", None, None),
        P("rx", "ry", None, None, None),
        P("rx", "ry", None, None, None),
    )
    out_specs = (P("rx", "ry", None, None, None), P("rx", "ry", None, None, None))
    return jax.shard_map(body, mesh=mesh, in_specs=in_specs, out_specs=out_specs, check_vma=False)
```

profile of v0, /device:TPU:2, one launch (start us, length us, event | category | flops | bytes accessed | tf_op | source)
XLA Modules:
  0.0 115.2 jit_solution(852307972325386525)
XLA Ops:
  0.6 1.3 %copy.7.level_ref = s32[1,1,4,2]{3,2,1,0:T(4,128)} copy(s32[1,1,4,2]{2,3,1,0:T(2,128)} %param.7) | data formatting | bytes 64 | tf_op args[2]
  2.0 108.4 %train.1 = (f32[9,192,192]{2,1,0:T(8,128)}, f32[9,192,192]{2,1,0:T(8,128)}) custom-call(s32[1,1,4,2]{3,2,1,0:T(4,128)} %copy.7.level_ref, bf16[1,1,4,2,192,1024]{5,4,3,2,1,0:T(8,128)(2,1)} %clean_hbm.1, bf16[1,1,4,2,192,1024]{5,4,3,2,1,0:T(8,128)(2,1)} %noise_hbm.1, f32[1,1,9,192,192]{4,3,2,1,0:T(8,128)} %w_hbm.1, f32[1,1,9,192,192]{4,3,2,1,0:T(8,128)} %v_hbm.1), custom_call_target="tpu_custom_call" | custom-call | tf_op jit(solution)/shard_map/train/pallas_call | solution.py:226
  110.4 0.0 copy-start
  110.4 3.0 %copy.8 = f32[1,1,9,192,192]{4,3,2,1,0:T(8,128)} copy(f32[1,1,9,192,192]{3,4,2,1,0:T(8,128)} %bitcast.7) | data formatting | bytes 2654208
  113.4 0.0 copy-done
  113.4 1.8 %copy.9 = f32[1,1,9,192,192]{4,3,2,1,0:T(8,128)} copy(f32[1,1,9,192,192]{3,4,2,1,0:T(8,128)S(1)} %bitcast.6) | data formatting | bytes 2654208
Async XLA Ops:
  110.4 3.0 %copy-start = (f32[9,192,192]{2,1,0:T(8,128)S(1)}, f32[9,192,192]{2,1,0:T(8,128)}, u32[]{:S(2)}) copy-start(f32[9,192,192]{2,1,0:T(8,128)} %get-tuple-element.5) | copy-start | bytes 3981316
where the time goes:
time: 115 us
  Pallas kernels  108 us (94%)
  local copies, waits for them, and re-layouts  6.16 us (5%)
    pallas_call x1, Pallas kernels, body(): pl.pallas_call(kernel, out_shape=(out, out), in_specs=[pl.BlockSpec(memor...  108 us
    unnamed x5, local copies, waits for them, and re-layouts  6.16 us

commit v1 on v0

v1 whole, which is shorter than its diff:
```python
import math

import jax
import jax.numpy as jnp
from jax import lax
from jax.experimental import pallas as pl
from jax.experimental.pallas import tpu as pltpu
from jax.sharding import PartitionSpec as P

RES = 32
CELLS = RES * RES
STEPS = 4
LEVELS = 32
C = 192
TAPS = 9
FAN = TAPS * C
OC = 16
HALF = OC // 2
ROWS = OC + HALF
UNITS = C // OC
CHUNKS = UNITS // 2 + 1
BATCH = 2
TILES = BATCH * CELLS // 128

norm_epsilon = 1e-05
momentum_decay = 0.9
learn_rate = 50.0
silu_scale = 0.596
MESH = pl.DeviceIdType.MESH
F32 = jnp.float32
BF16 = jnp.bfloat16


def partner_of(step):
    rx, ry = lax.axis_index("rx"), lax.axis_index("ry")
    odd = step % 2
    bit_x = (8 - 2 * step) * (1 - odd)
    bit_y = (10 - 2 * step) * odd
    px = rx + bit_x * (1 - 2 * ((rx // (bit_x + odd)) % 2))
    py = ry + bit_y * (1 - 2 * ((ry // (bit_y + 1 - odd)) % 2))
    return {"rx": px, "ry": py}


def pack(full):
    rest = full[:, :, 128:]
    return full[:, :, :128], jnp.concatenate([rest[:, :HALF], rest[:, HALF:]], axis=-1)


def unpack(packed):
    rest = packed[:, OC:]
    rest = jnp.concatenate([rest[:, :, :64], pltpu.roll(rest, 64, 2)[:, :, :64]], axis=1)
    return jnp.concatenate([packed[:, :OC], rest], axis=-1)


def kernel(
    level_ref, clean_hbm, noise_hbm, w_hbm, v_hbm, new_w_hbm, new_v_hbm,
    clean, noise, w_in, v_in, clean_p, x_ref, xt_ref, mine, other, vel, w_out,
    in_sem, wv_sem, out_sem, send_sem, recv_sem,
):
    pltpu.make_async_copy(w_hbm.at[0, 0], w_in, wv_sem.at[0]).start()
    pltpu.make_async_copy(v_hbm.at[0, 0], v_in, wv_sem.at[1]).start()
    for step in range(STEPS):
        pltpu.make_async_copy(clean_hbm.at[0, 0, step], clean.at[step], in_sem.at[0, step]).start()
        pltpu.make_async_copy(noise_hbm.at[0, 0, step], noise.at[step], in_sem.at[1, step]).start()

    barrier = pltpu.get_barrier_semaphore()
    for step in range(STEPS):
        pl.semaphore_signal(barrier, inc=1, device_id=partner_of(step), device_id_type=MESH)

    pltpu.make_async_copy(w_hbm.at[0, 0], w_in, wv_sem.at[0]).wait()
    pltpu.make_async_copy(v_hbm.at[0, 0], v_in, wv_sem.at[1]).wait()

    def turn(tap, carry):
        wt = jnp.transpose(w_in[tap])
        rest = wt[:, 128:].reshape(UNITS, 2, HALF, 64)
        rest = jnp.concatenate([rest[:, 0], rest[:, 1]], axis=-1)
        for slot in (mine, other):
            slot[0, :, tap, :OC, :] = wt[:, :128].reshape(UNITS, OC, 128)
            slot[0, :, tap, OC:, :] = rest
        vel[tap] = jnp.transpose(v_in[tap])
        return carry

    lax.fori_loop(0, TAPS, turn, 0)

    pl.semaphore_wait(barrier, STEPS)

    lane = lax.broadcasted_iota(jnp.int32, (1, 128), 1)
    low64, low32 = lane < 64, lane % 64 < 32
    col = lane % RES
    ok_col = {-1: col > 0, 1: col < RES - 1}
    ok_row = {-1: lane >= RES, 1: lane < 128 - RES}

    def regroup(tiles):
        out = [None] * 8
        for u in range(4):
            lo, hi = tiles[u], tiles[u + 4]
            out[u] = jnp.where(low64, lo, pltpu.roll(hi, 64, 1))
            out[u + 4] = jnp.where(low64, pltpu.roll(lo, 64, 1), hi)
        last = [None] * 8
        for high in range(2):
            for low in range(2):
                lo, hi = out[4 * high + low], out[4 * high + 2 + low]
                last[4 * low + 2 * high] = jnp.where(low32, lo, pltpu.roll(hi, 32, 1))
                last[4 * low + 2 * high + 1] = jnp.where(low32, pltpu.roll(lo, 96, 1), hi)
        return last

    def prepare(step):
        pltpu.make_async_copy(clean_hbm.at[0, 0, step], clean.at[step], in_sem.at[0, step]).wait()
        pltpu.make_async_copy(noise_hbm.at[0, 0, step], noise.at[step], in_sem.at[1, step]).wait()
        for b in range(BATCH):
            level = jnp.full((1, 128), level_ref[0, 0, b, step].astype(F32), F32)
            sigma = 0.2 * jnp.exp(level * (math.log(25.0) / (LEVELS - 1)))
            c_in = 1.0 / jnp.sqrt(sigma * sigma + 0.25)

            def block(i, carry):
                at = pl.ds(pl.multiple_of(i * 96, 96), 96)
                pair = [
                    regroup([ref[step, b, at, 128 * u : 128 * u + 128] for u in range(8)])
                    for ref in (clean, noise)
                ]
                for v in range(8):
                    to = 128 * (8 * b + v)
                    clean_p[step, at, to : to + 128] = pair[0][v]
                    noisy = c_in * (pair[0][v].astype(F32) + sigma * pair[1][v].astype(F32))
                    x_ref[step, at, to : to + 128] = noisy.astype(BF16)
                return carry

            lax.fori_loop(0, C // 96, block, 0)

        def turn_block(i, carry):
            at = pl.ds(pl.multiple_of(i * 128, 128), 128)
            xt_ref[step, at, :] = jnp.transpose(x_ref[step, :, at])
            return carry

        lax.fori_loop(0, TILES, turn_block, 0, unroll=True)

    def exchange(step, unit):
        return pltpu.make_async_remote_copy(
            src_ref=mine.at[step + 1, unit],
            dst_ref=other.at[step + 1, unit],
            send_sem=send_sem.at[step, unit],
            recv_sem=recv_sem.at[step, unit],
            device_id=partner_of(step),
            device_id_type=MESH,
        )

    def average(step, unit, units):
        both = [unpack(0.5 * (mine[step, unit + i] + other[step, unit + i])) for i in range(units)]
        return jnp.concatenate(both, axis=1)

    def task(step, unit, units):
        width = OC * units
        at = pl.ds(pl.multiple_of(unit * OC, OC), width)

        @pl.when(step > 0)
        def _():
            for i in range(units):
                exchange(step - 1, unit + i).wait_recv()

        w = average(step, unit, units)
        square = jnp.sum(jnp.sum(w * w, axis=0), axis=1, keepdims=True)
        radius = jnp.sqrt(square / FAN + norm_epsilon)
        scale = 1.0 / (radius * math.sqrt(FAN))
        lhs = (w * scale).astype(BF16).reshape(TAPS * width, C)
        y = jnp.dot(lhs, x_ref[step], preferred_element_type=F32)
        pieces = {}
        for b in range(BATCH):

            def tap(dy, dx, v):
                t, to = 3 * (dy + 1) + dx + 1, 128 * (8 * b + (v + dy) % 8)
                part = y[t * width : (t + 1) * width, to : to + 128]
                if 0 <= v + dy < 8:
                    return part
                return jnp.where(ok_row[dy], pltpu.roll(part, -RES * dy % 128, 1), 0.0)

            moved = {}
            for v in range(8):
                to = 128 * (8 * b + v)
                part = {dx: tap(0, dx, v) + tap(-1, dx, v) + tap(1, dx, v) for dx in (-1, 0, 1)}
                z = part[0]
                for dx in (-1, 1):
                    z = z + jnp.where(ok_col[dx], pltpu.roll(part[dx], -dx % 128, 1), 0.0)
                sig = 1.0 / (1.0 + jnp.exp(-z))
                error = z * sig * (1.0 / silu_scale) - clean_p[step, at, to : to + 128].astype(F32)
                dz = error * sig * (1.0 + z * (1.0 - sig)) * (2.0 / (silu_scale * BATCH * CELLS))
                moved[0, v] = dz = dz.astype(BF16)
                for dx in (-1, 1):
                    moved[dx, v] = jnp.where(
                        ok_col[-dx], pltpu.roll(dz, dx % 128, 1), jnp.zeros((), BF16)
                    )
            for v in range(8):
                for dx in (-1, 0, 1):
                    for dy in (-1, 0, 1):
                        piece = moved[dx, (v - dy) % 8]
                        if not 0 <= v - dy < 8:
                            piece = jnp.where(
                                ok_row[-dy], pltpu.roll(piece, RES * dy % 128, 1), jnp.zeros((), BF16)
                            )
                        pieces[dy, dx, 8 * b + v] = piece
        rows = jnp.concatenate(
            [
                jnp.concatenate([pieces[dy, dx, v] for v in range(TILES)], axis=1)
                for dy in (-1, 0, 1)
                for dx in (-1, 0, 1)
            ],
            axis=0,
        )
        grad_eff = jnp.dot(rows, xt_ref[step], preferred_element_type=F32)
        grad_eff = grad_eff.reshape(TAPS, width, C)
        inner = jnp.sum(jnp.sum(grad_eff * w, axis=0), axis=1, keepdims=True)
        back = inner / (FAN * math.sqrt(FAN) * (radius * radius * radius))
        grad = grad_eff * scale - w * back
        v = momentum_decay * vel[:, at, :] + learn_rate * grad
        vel[:, at, :] = v
        local = w - v
        for i in range(units):
            first, rest = pack(local[:, i * OC : (i + 1) * OC])
            mine[step + 1, unit + i, :, :OC, :] = first
            mine[step + 1, unit + i, :, OC:, :] = rest
            exchange(step, unit + i).start()

        @pl.when(step == STEPS - 1)
        def _():
            for i in range(units):
                write(vel, new_v_hbm, 1, unit + i).start()

    def write(src, dst, which, unit):
        at = pl.multiple_of(unit * OC, OC)
        return pltpu.make_async_copy(
            src.at[:, pl.ds(at, OC), :], dst.at[:, pl.ds(at, OC), :], out_sem.at[which, unit]
        )

    def finish(unit, units):
        for i in range(units):
            exchange(STEPS - 1, unit + i).wait_recv()
        w_out[:, pl.ds(pl.multiple_of(unit * OC, OC), OC * units), :] = average(STEPS, unit, units)
        for i in range(units):
            write(w_out, new_w_hbm, 0, unit + i).start()

    def on_chunk(chunk, do):
        unit = 2 * chunk - (chunk + CHUNKS - 1) // CHUNKS

        @pl.when((chunk == 0) | (chunk == CHUNKS - 1))
        def _():
            do(unit, 1)

        @pl.when((chunk > 0) & (chunk < CHUNKS - 1))
        def _():
            do(unit, 2)

    def wave(i, carry):
        k = i - 1

        def inner(step, carry):
            on_chunk(k - step - step // 2, lambda unit, units: task(step, unit, units))
            early = (step == 0) & (k == 1)
            late = (step == STEPS - 1) & ((k == -1) | (k == 1) | (k == 2))

            @pl.when(early | late)
            def _():
                prepare(k + step // (STEPS - 1))

            return carry

        lax.fori_loop(0, STEPS, inner, 0)
        on_chunk(k - 5, finish)
        return carry

    lax.fori_loop(0, CHUNKS + 6, wave, 0)

    def drain(unit, carry):
        for step in range(STEPS):
            exchange(step, unit).wait_send()
        write(w_out, new_w_hbm, 0, unit).wait()
        write(vel, new_v_hbm, 1, unit).wait()
        return carry

    lax.fori_loop(0, UNITS, drain, 0)


def body(clean, noise, noise_level, weight, velocity):
    hbm = pl.BlockSpec(memory_space=pl.ANY)
    out = jax.ShapeDtypeStruct((TAPS, C, C), F32)
    new_w, new_v = pl.pallas_call(
        kernel,
        out_shape=(out, out),
        in_specs=[pl.BlockSpec(memory_space=pltpu.SMEM), hbm, hbm, hbm, hbm],
        out_specs=(hbm, hbm),
        scratch_shapes=[
            pltpu.VMEM((STEPS, BATCH, C, CELLS), BF16),
            pltpu.VMEM((STEPS, BATCH, C, CELLS), BF16),
            pltpu.VMEM((TAPS, C, C), F32),
            pltpu.VMEM((TAPS, C, C), F32),
            pltpu.VMEM((STEPS, C, BATCH * CELLS), BF16),
            pltpu.VMEM((STEPS, C, BATCH * CELLS), BF16),
            pltpu.VMEM((STEPS, BATCH * CELLS, C), BF16),
            pltpu.VMEM((STEPS + 1, UNITS, TAPS, ROWS, 128), F32),
            pltpu.VMEM((STEPS + 1, UNITS, TAPS, ROWS, 128), F32),
            pltpu.VMEM((TAPS, C, C), F32),
            pltpu.VMEM((TAPS, C, C), F32),
            pltpu.SemaphoreType.DMA((2, STEPS)),
            pltpu.SemaphoreType.DMA((2,)),
            pltpu.SemaphoreType.DMA((2, UNITS)),
            pltpu.SemaphoreType.DMA((STEPS, UNITS)),
            pltpu.SemaphoreType.DMA((STEPS, UNITS)),
        ],
        compiler_params=pltpu.CompilerParams(
            collective_id=0, has_side_effects=True, vmem_limit_bytes=58 << 20
        ),
        name="train",
    )(jnp.swapaxes(noise_level, 2, 3), clean, noise, weight, velocity)
    return (
        jnp.swapaxes(new_w, 1, 2)[None, None],
        jnp.swapaxes(new_v, 1, 2)[None, None],
    )


def solution(mesh):
    in_specs = (
        P("rx", "ry", None, None, None, None),
        P("rx", "ry", None, None, None, None),
        P("rx", "ry", None, None),
        P("rx", "ry", None, None, None),
        P("rx", "ry", None, None, None),
    )
    out_specs = (P("rx", "ry", None, None, None), P("rx", "ry", None, None, None))
    return jax.shard_map(body, mesh=mesh, in_specs=in_specs, out_specs=out_specs, check_vma=False)
```

time: 115 us -> 107 us (0.930)
  the two profiles are of different devices: /device:TPU:2 before, /device:TPU:8 now
where the time goes in v1:
time: 107 us
  Pallas kernels  101 us (94%)
  local copies, waits for them, and re-layouts  4.82 us (5%)
    pallas_call x1, Pallas kernels, body(): pl.pallas_call(kernel, out_shape=(out, out), in_specs=[pl.BlockSpec(memor...  101 us
    unnamed x4, local copies, waits for them, and re-layouts  4.82 us

profile of v1, /device:TPU:8, one launch (start us, length us, event | category | flops | bytes accessed | tf_op | source)
XLA Modules:
  0.0 106.6 jit_solution(15588153771789396336)
XLA Ops:
  0.6 101.1 %train.1 = (f32[9,192,192]{2,1,0:T(8,128)}, f32[9,192,192]{2,1,0:T(8,128)}) custom-call(s32[1,1,2,4]{3,2,1,0:T(2,128)} %bitcast.9, bf16[1,1,4,2,192,1024]{5,4,3,2,1,0:T(8,128)(2,1)} %clean_hbm.1, bf16[1,1,4,2,192,1024]{5,4,3,2,1,0:T(8,128)(2,1)} %noise_hbm.1, f32[1,1,9,192,192]{4,3,2,1,0:T(8,128)} %w_hbm.1, f32[1,1,9,192,192]{4,3,2,1,0:T(8,128)} %v_hbm.1), custom_call_target="tpu_custom_call" | custom-call | tf_op jit(solution)/shard_map/train/pallas_call | solution.py:284
  101.8 0.0 copy-start
  101.8 3.0 %copy.7 = f32[1,1,9,192,192]{4,3,2,1,0:T(8,128)} copy(f32[1,1,9,192,192]{3,4,2,1,0:T(8,128)} %bitcast.8) | data formatting | bytes 2654208
  104.8 0.0 copy-done
  104.8 1.8 %copy.8 = f32[1,1,9,192,192]{4,3,2,1,0:T(8,128)} copy(f32[1,1,9,192,192]{3,4,2,1,0:T(8,128)S(1)} %bitcast.7) | data formatting | bytes 2654208
Async XLA Ops:
  101.8 3.0 %copy-start = (f32[9,192,192]{2,1,0:T(8,128)S(1)}, f32[9,192,192]{2,1,0:T(8,128)}, u32[]{:S(2)}) copy-start(f32[9,192,192]{2,1,0:T(8,128)} %get-tuple-element.5) | copy-start | bytes 3981316

commit v2 on v1

--- a/solution.py
+++ b/solution.py
@@ -18,7 +18,9 @@
 HALF = OC // 2
 ROWS = OC + HALF
 UNITS = C // OC
-CHUNKS = UNITS // 2 + 1
+DOUBLES = 4
+CHUNKS = UNITS - DOUBLES
+LAST_LAG = 6
 BATCH = 2
 TILES = BATCH * CELLS // 128
 
@@ -53,22 +55,24 @@
 
 
 def kernel(
-    level_ref, clean_hbm, noise_hbm, w_hbm, v_hbm, new_w_hbm, new_v_hbm,
+    level_ref, clean_hbm, noise_hbm, w_hbm, v_hbm, new_w, new_v,
     clean, noise, w_in, v_in, clean_p, x_ref, xt_ref, mine, other, vel, w_out,
-    in_sem, wv_sem, out_sem, send_sem, recv_sem,
+    in_sem, wv_sem, send_sem, recv_sem,
 ):
-    pltpu.make_async_copy(w_hbm.at[0, 0], w_in, wv_sem.at[0]).start()
-    pltpu.make_async_copy(v_hbm.at[0, 0], v_in, wv_sem.at[1]).start()
-    for step in range(STEPS):
-        pltpu.make_async_copy(clean_hbm.at[0, 0, step], clean.at[step], in_sem.at[0, step]).start()
-        pltpu.make_async_copy(noise_hbm.at[0, 0, step], noise.at[step], in_sem.at[1, step]).start()
+    def load(step):
+        return (
+            pltpu.make_async_copy(clean_hbm.at[0, 0, step], clean.at[step], in_sem.at[0, step]),
+            pltpu.make_async_copy(noise_hbm.at[0, 0, step], noise.at[step], in_sem.at[1, step]),
+        )
+
+    load_w = pltpu.make_async_copy(w_hbm.at[0, 0], w_in, wv_sem.at[0])
+    load_v = pltpu.make_async_copy(v_hbm.at[0, 0], v_in, wv_sem.at[1])
+    for copy in load(0) + (load_w, load_v):
+        copy.start()
 
     barrier = pltpu.get_barrier_semaphore()
     for step in range(STEPS):
         pl.semaphore_signal(barrier, inc=1, device_id=partner_of(step), device_id_type=MESH)
-
-    pltpu.make_async_copy(w_hbm.at[0, 0], w_in, wv_sem.at[0]).wait()
-    pltpu.make_async_copy(v_hbm.at[0, 0], v_in, wv_sem.at[1]).wait()
 
     def turn(tap, carry):
         wt = jnp.transpose(w_in[tap])
@@ -79,10 +83,6 @@
             slot[0, :, tap, OC:, :] = rest
         vel[tap] = jnp.transpose(v_in[tap])
         return carry
-
-    lax.fori_loop(0, TAPS, turn, 0)
-
-    pl.semaphore_wait(barrier, STEPS)
 
     lane = lax.broadcasted_iota(jnp.int32, (1, 128), 1)
     low64, low32 = lane < 64, lane % 64 < 32
@@ -105,27 +105,22 @@
         return last
 
     def prepare(step):
-        pltpu.make_async_copy(clean_hbm.at[0, 0, step], clean.at[step], in_sem.at[0, step]).wait()
-        pltpu.make_async_copy(noise_hbm.at[0, 0, step], noise.at[step], in_sem.at[1, step]).wait()
+        for copy in load(step):
+            copy.wait()
         for b in range(BATCH):
             level = jnp.full((1, 128), level_ref[0, 0, b, step].astype(F32), F32)
             sigma = 0.2 * jnp.exp(level * (math.log(25.0) / (LEVELS - 1)))
             c_in = 1.0 / jnp.sqrt(sigma * sigma + 0.25)
 
-            def block(i, carry):
-                at = pl.ds(pl.multiple_of(i * 96, 96), 96)
-                pair = [
-                    regroup([ref[step, b, at, 128 * u : 128 * u + 128] for u in range(8)])
-                    for ref in (clean, noise)
-                ]
-                for v in range(8):
-                    to = 128 * (8 * b + v)
-                    clean_p[step, at, to : to + 128] = pair[0][v]
-                    noisy = c_in * (pair[0][v].astype(F32) + sigma * pair[1][v].astype(F32))
-                    x_ref[step, at, to : to + 128] = noisy.astype(BF16)
-                return carry
-
-            lax.fori_loop(0, C // 96, block, 0)
+            pair = [
+                regroup([ref[step, b, :, 128 * u : 128 * u + 128] for u in range(8)])
+                for ref in (clean, noise)
+            ]
+            for v in range(8):
+                to = 128 * (8 * b + v)
+                clean_p[step, :, to : to + 128] = pair[0][v]
+                noisy = c_in * (pair[0][v].astype(F32) + sigma * pair[1][v].astype(F32))
+                x_ref[step, :, to : to + 128] = noisy.astype(BF16)
 
         def turn_block(i, carry):
             at = pl.ds(pl.multiple_of(i * 128, 128), 128)
@@ -133,6 +128,15 @@
             return carry
 
         lax.fori_loop(0, TILES, turn_block, 0, unroll=True)
+
+    prepare(0)
+    load_w.wait()
+    load_v.wait()
+    lax.fori_loop(0, TAPS, turn, 0, unroll=True)
+    for step in range(1, STEPS):
+        for copy in load(step):
+            copy.start()
+    pl.semaphore_wait(barrier, STEPS)
 
     def exchange(step, unit):
         return pltpu.make_async_remote_copy(
@@ -219,60 +223,58 @@
             mine[step + 1, unit + i, :, OC:, :] = rest
             exchange(step, unit + i).start()
 
-        @pl.when(step == STEPS - 1)
-        def _():
-            for i in range(units):
-                write(vel, new_v_hbm, 1, unit + i).start()
-
-    def write(src, dst, which, unit):
-        at = pl.multiple_of(unit * OC, OC)
-        return pltpu.make_async_copy(
-            src.at[:, pl.ds(at, OC), :], dst.at[:, pl.ds(at, OC), :], out_sem.at[which, unit]
-        )
-
     def finish(unit, units):
         for i in range(units):
             exchange(STEPS - 1, unit + i).wait_recv()
         w_out[:, pl.ds(pl.multiple_of(unit * OC, OC), OC * units), :] = average(STEPS, unit, units)
-        for i in range(units):
-            write(w_out, new_w_hbm, 0, unit + i).start()
 
     def on_chunk(chunk, do):
-        unit = 2 * chunk - (chunk + CHUNKS - 1) // CHUNKS
-
-        @pl.when((chunk == 0) | (chunk == CHUNKS - 1))
+        unit = jnp.minimum(2 * chunk - (chunk + CHUNKS - 1) // CHUNKS, chunk + DOUBLES)
+
+        @pl.when((chunk == 0) | ((chunk > DOUBLES) & (chunk < CHUNKS)))
         def _():
             do(unit, 1)
 
-        @pl.when((chunk > 0) & (chunk < CHUNKS - 1))
+        @pl.when((chunk > 0) & (chunk <= DOUBLES))
         def _():
             do(unit, 2)
 
-    def wave(i, carry):
-        k = i - 1
-
+    def wave(k, carry):
         def inner(step, carry):
-            on_chunk(k - step - step // 2, lambda unit, units: task(step, unit, units))
-            early = (step == 0) & (k == 1)
-            late = (step == STEPS - 1) & ((k == -1) | (k == 1) | (k == 2))
-
-            @pl.when(early | late)
+            chunk = k - step - step // 2
+
+            @pl.when((chunk == 0) & (step > 0))
             def _():
-                prepare(k + step // (STEPS - 1))
-
+                prepare(step)
+
+            on_chunk(chunk, lambda unit, units: task(step, unit, units))
             return carry
 
         lax.fori_loop(0, STEPS, inner, 0)
-        on_chunk(k - 5, finish)
+
+        @pl.when(k == CHUNKS + LAST_LAG - 2)
+        def _():
+            def turn_back(tap, carry):
+                new_v[tap] = jnp.transpose(vel[tap])
+                new_w[tap, :, :128] = jnp.transpose(w_out[tap, :128])
+                return carry
+
+            lax.fori_loop(0, TAPS, turn_back, 0)
+
+        on_chunk(k - LAST_LAG, finish)
         return carry
 
-    lax.fori_loop(0, CHUNKS + 6, wave, 0)
+    lax.fori_loop(0, CHUNKS + LAST_LAG, wave, 0)
+
+    def turn_rest(tap, carry):
+        new_w[tap, :, 128:] = jnp.transpose(w_out[tap, 128:])
+        return carry
+
+    lax.fori_loop(0, TAPS, turn_rest, 0, unroll=True)
 
     def drain(unit, carry):
         for step in range(STEPS):
             exchange(step, unit).wait_send()
-        write(w_out, new_w_hbm, 0, unit).wait()
-        write(vel, new_v_hbm, 1, unit).wait()
         return carry
 
     lax.fori_loop(0, UNITS, drain, 0)
@@ -280,12 +282,13 @@
 
 def body(clean, noise, noise_level, weight, velocity):
     hbm = pl.BlockSpec(memory_space=pl.ANY)
-    out = jax.ShapeDtypeStruct((TAPS, C, C), F32)
+    out = pltpu.VMEM((TAPS, C, C), F32)
+    vmem = pl.BlockSpec(memory_space=pltpu.VMEM)
     new_w, new_v = pl.pallas_call(
         kernel,
         out_shape=(out, out),
         in_specs=[pl.BlockSpec(memory_space=pltpu.SMEM), hbm, hbm, hbm, hbm],
-        out_specs=(hbm, hbm),
+        out_specs=(vmem, vmem),
         scratch_shapes=[
             pltpu.VMEM((STEPS, BATCH, C, CELLS), BF16),
             pltpu.VMEM((STEPS, BATCH, C, CELLS), BF16),
@@ -300,19 +303,15 @@
             pltpu.VMEM((TAPS, C, C), F32),
             pltpu.SemaphoreType.DMA((2, STEPS)),
             pltpu.SemaphoreType.DMA((2,)),
-            pltpu.SemaphoreType.DMA((2, UNITS)),
             pltpu.SemaphoreType.DMA((STEPS, UNITS)),
             pltpu.SemaphoreType.DMA((STEPS, UNITS)),
         ],
         compiler_params=pltpu.CompilerParams(
-            collective_id=0, has_side_effects=True, vmem_limit_bytes=58 << 20
+            collective_id=0, has_side_effects=True, vmem_limit_bytes=52 << 20
         ),
         name="train",
     )(jnp.swapaxes(noise_level, 2, 3), clean, noise, weight, velocity)
-    return (
-        jnp.swapaxes(new_w, 1, 2)[None, None],
-        jnp.swapaxes(new_v, 1, 2)[None, None],
-    )
+    return (new_w[None, None], new_v[None, None])
 
 
 def solution(mesh):

time: 107 us -> 96.5 us (0.902)
  the two profiles are of different devices: /device:TPU:8 before, /device:TPU:96 now
where the time goes in v2:
time: 96.5 us; the launch traced here: 96.4 us
  Pallas kernels  93.3 us (97%)
  local copies, waits for them, and re-layouts  2.42 us (3%)
    pallas_call x1, Pallas kernels, body(): pl.pallas_call(kernel, out_shape=(out, out), in_specs=[pl.BlockSpec(memor...  93.3 us
    unnamed x2, local copies, waits for them, and re-layouts  2.42 us

profile of v2, /device:TPU:96, one launch (start us, length us, event | category | flops | bytes accessed | tf_op | source)
XLA Modules:
  0.0 96.4 jit_solution(9481512449430050706)
XLA Ops:
  0.6 93.3 %train.1 = (f32[9,192,192]{2,1,0:T(8,128)S(1)}, f32[9,192,192]{2,1,0:T(8,128)S(1)}) custom-call(s32[1,1,2,4]{3,2,1,0:T(2,128)} %bitcast.5, bf16[1,1,4,2,192,1024]{5,4,3,2,1,0:T(8,128)(2,1)} %clean_hbm.1, bf16[1,1,4,2,192,1024]{5,4,3,2,1,0:T(8,128)(2,1)} %noise_hbm.1, f32[1,1,9,192,192]{4,3,2,1,0:T(8,128)} %w_hbm.1, f32[1,1,9,192,192]{4,3,2,1,0:T(8,128)} %v_hbm.1), custom_call_target="tpu_custom_call" | custom-call | tf_op jit(solution)/shard_map/train/pallas_call | solution.py:287
  94.0 1.2 %copy.9 = f32[1,1,9,192,192]{4,3,2,1,0:T(8,128)} copy(f32[1,1,9,192,192]{4,3,2,1,0:T(8,128)S(1)} %bitcast.4) | data formatting | bytes 2654208
  95.2 1.2 %copy.10 = f32[1,1,9,192,192]{4,3,2,1,0:T(8,128)} copy(f32[1,1,9,192,192]{4,3,2,1,0:T(8,128)S(1)} %bitcast.3) | data formatting | bytes 2654208

commit v3 on v2

--- a/solution.py
+++ b/solution.py
@@ -239,6 +239,11 @@
         def _():
             do(unit, 2)
 
+    def drain(unit, carry):
+        for step in range(STEPS):
+            exchange(step, unit).wait_send()
+        return carry
+
     def wave(k, carry):
         def inner(step, carry):
             chunk = k - step - step // 2
@@ -261,6 +266,10 @@
 
             lax.fori_loop(0, TAPS, turn_back, 0)
 
+        @pl.when(k == CHUNKS + LAST_LAG - 1)
+        def _():
+            lax.fori_loop(0, UNITS, drain, 0)
+
         on_chunk(k - LAST_LAG, finish)
         return carry
 
@@ -272,12 +281,16 @@
 
     lax.fori_loop(0, TAPS, turn_rest, 0, unroll=True)
 
-    def drain(unit, carry):
-        for step in range(STEPS):
-            exchange(step, unit).wait_send()
-        return carry
-
-    lax.fori_loop(0, UNITS, drain, 0)
+
+def store(new_w, new_v, w_hbm, v_hbm, sem):
+    copies = (
+        pltpu.make_async_copy(new_w, w_hbm.at[0, 0], sem.at[0]),
+        pltpu.make_async_copy(new_v, v_hbm.at[0, 0], sem.at[1]),
+    )
+    for copy in copies:
+        copy.start()
+    for copy in copies:
+        copy.wait()
 
 
 def body(clean, noise, noise_level, weight, velocity):
@@ -311,7 +324,15 @@
         ),
         name="train",
     )(jnp.swapaxes(noise_level, 2, 3), clean, noise, weight, velocity)
-    return (new_w[None, None], new_v[None, None])
+    shape = jax.ShapeDtypeStruct((1, 1, TAPS, C, C), F32)
+    return pl.pallas_call(
+        store,
+        out_shape=(shape, shape),
+        in_specs=[vmem, vmem],
+        out_specs=(hbm, hbm),
+        scratch_shapes=[pltpu.SemaphoreType.DMA((2,))],
+        name="store",
+    )(pltpu.with_memory_space_constraint(new_w, pltpu.VMEM), pltpu.with_memory_space_constraint(new_v, pltpu.VMEM))
 
 
 def solution(mesh):

time: 96.5 us -> 95.8 us (level)
  local copies, waits for them, and re-layouts: 2.42 us -> 0 us
  Pallas kernels: 93.3 us -> 95 us
    unnamed x2 -> x0, local copies, waits for them, and re-layouts: 2.42 us -> none
    pallas_call x0 -> x1, Pallas kernels: none -> 1.81 us  [body(): pl.pallas_call(store, out_shape=(shape, shape), in_specs=[vmem, vmem], ou...]
where the time goes in v3:
time: 95.8 us; the launch traced here: 95.7 us
  Pallas kernels  95 us (99%)
    pallas_call x1, Pallas kernels, body(): pl.pallas_call(kernel, out_shape=(out, out), in_specs=[pl.BlockSpec(memor...  93.2 us

profile of v3, /device:TPU:96, one launch (start us, length us, event | category | flops | bytes accessed | tf_op | source)
XLA Modules:
  0.0 95.7 jit_solution(10480779939542236156)
XLA Ops:
  0.6 93.2 %train.1 = (f32[9,192,192]{2,1,0:T(8,128)S(1)}, f32[9,192,192]{2,1,0:T(8,128)S(1)}) custom-call(s32[1,1,2,4]{3,2,1,0:T(2,128)} %bitcast.1, bf16[1,1,4,2,192,1024]{5,4,3,2,1,0:T(8,128)(2,1)} %clean_hbm.1, bf16[1,1,4,2,192,1024]{5,4,3,2,1,0:T(8,128)(2,1)} %noise_hbm.1, f32[1,1,9,192,192]{4,3,2,1,0:T(8,128)} %w_hbm.1, f32[1,1,9,192,192]{4,3,2,1,0:T(8,128)} %v_hbm.1), custom_call_target="tpu_custom_call" | custom-call | tf_op jit(solution)/shard_map/train/pallas_call | solution.py:300
  93.9 1.8 %store.1 = (f32[1,1,9,192,192]{4,3,2,1,0:T(8,128)}, f32[1,1,9,192,192]{4,3,2,1,0:T(8,128)}) custom-call(f32[9,192,192]{2,1,0:T(8,128)S(1)} %get-tuple-element.4.new_w, f32[9,192,192]{2,1,0:T(8,128)S(1)} %get-tuple-element.5.new_v), custom_call_target="tpu_custom_call" | custom-call | tf_op jit(solution)/shard_map/store/pallas_call | solution.py:328

commit v4 on v3

--- a/solution.py
+++ b/solution.py
@@ -122,6 +122,7 @@
                 noisy = c_in * (pair[0][v].astype(F32) + sigma * pair[1][v].astype(F32))
                 x_ref[step, :, to : to + 128] = noisy.astype(BF16)
 
+    def turn_inputs(step):
         def turn_block(i, carry):
             at = pl.ds(pl.multiple_of(i * 128, 128), 128)
             xt_ref[step, at, :] = jnp.transpose(x_ref[step, :, at])
@@ -132,6 +133,7 @@
     prepare(0)
     load_w.wait()
     load_v.wait()
+    turn_inputs(0)
     lax.fori_loop(0, TAPS, turn, 0, unroll=True)
     for step in range(1, STEPS):
         for copy in load(step):
@@ -251,6 +253,7 @@
             @pl.when((chunk == 0) & (step > 0))
             def _():
                 prepare(step)
+                turn_inputs(step)
 
             on_chunk(chunk, lambda unit, units: task(step, unit, units))
             return carry
@@ -264,7 +267,7 @@
                 new_w[tap, :, :128] = jnp.transpose(w_out[tap, :128])
                 return carry
 
-            lax.fori_loop(0, TAPS, turn_back, 0)
+            lax.fori_loop(0, TAPS, turn_back, 0, unroll=True)
 
         @pl.when(k == CHUNKS + LAST_LAG - 1)
         def _():

time: 95.8 us -> 95.6 us (level)
  no operation moved by 1% of the time
where the time goes in v4:
time: 95.6 us; the launch traced here: 95.5 us
  Pallas kernels  94.9 us (99%)
    pallas_call x1, Pallas kernels, body(): pl.pallas_call(kernel, out_shape=(out, out), in_specs=[pl.BlockSpec(memor...  93.1 us

profile of v4, /device:TPU:96, one launch (start us, length us, event | category | flops | bytes accessed | tf_op | source)
XLA Modules:
  0.0 95.5 jit_solution(1509223581264706044)
XLA Ops:
  0.6 93.1 %train.1 = (f32[9,192,192]{2,1,0:T(8,128)S(1)}, f32[9,192,192]{2,1,0:T(8,128)S(1)}) custom-call(s32[1,1,2,4]{3,2,1,0:T(2,128)} %bitcast.1, bf16[1,1,4,2,192,1024]{5,4,3,2,1,0:T(8,128)(2,1)} %clean_hbm.1, bf16[1,1,4,2,192,1024]{5,4,3,2,1,0:T(8,128)(2,1)} %noise_hbm.1, f32[1,1,9,192,192]{4,3,2,1,0:T(8,128)} %w_hbm.1, f32[1,1,9,192,192]{4,3,2,1,0:T(8,128)} %v_hbm.1), custom_call_target="tpu_custom_call" | custom-call | tf_op jit(solution)/shard_map/train/pallas_call | solution.py:303
  93.7 1.8 %store.1 = (f32[1,1,9,192,192]{4,3,2,1,0:T(8,128)}, f32[1,1,9,192,192]{4,3,2,1,0:T(8,128)}) custom-call(f32[9,192,192]{2,1,0:T(8,128)S(1)} %get-tuple-element.4.new_w, f32[9,192,192]{2,1,0:T(8,128)S(1)} %get-tuple-element.5.new_v), custom_call_target="tpu_custom_call" | custom-call | tf_op jit(solution)/shard_map/store/pallas_call | solution.py:331
